TPU v7x, 256 devices: a whole 4x4x8 slice. The times are simulated.
256 devices in a mesh: row: 32 (over x, z), col: 8 (over y, core).
Axes of the slice: x: 4, y: 4, z: 8, core: 2. Of those that a mesh axis runs over, the one named last changes fastest.
Arguments:
- panel_block: float32 [16384, 128], P('row'), may hold values from -8 to 8, as said below
- trailing: float32 [16384, 16384], P('row', 'col'), may hold values from -80 to 80
Outputs:
- reduced: float32 [16384, 16384], P('row', 'col')
- band_block: float32 [128, 128], replicated
- first_factor: float32 [128, 128], replicated
Inputs may be any that keep to these rules, and one draw needn't show every extreme that they name: `panel_block`: entries of order the inverse square root of 16384; rows may differ in scale; the columns may be nearly dependent, with a condition number of the panel up to a few thousand; the first 128 rows of the orthonormal basis have spectral norm at most 0.8, so that I + top^T needs no pivoting.
All inputs are finite; a program needn't handle non-finite values.
Results may differ from a plain program's by a relative error of at most 0.0017.
Values sent between devices are 32-bit elements; how exact they have to be, the bound alone decides.
A program may use at most 128 MiB of HBM per device.

v0:
```python
import jax
import jax.numpy as jnp
from jax import lax
from jax.sharding import PartitionSpec as P

HIGH = lax.Precision.HIGHEST


def broadcast(shard, axis, root):
    mine = lax.axis_index(axis) == root
    return lax.psum(jnp.where(mine, shard, jnp.zeros_like(shard)), axis)


def gram_of(values):
    return lax.dot_general(
        values, values, (((0,), (0,)), ((), ())), precision=HIGH, preferred_element_type=jnp.float32
    )


def times_of(left, right):
    return jnp.dot(left, right, precision=HIGH, preferred_element_type=jnp.float32)


def outer_of(left, right):
    return lax.dot_general(
        left, right, (((1,), (1,)), ((), ())), precision=HIGH, preferred_element_type=jnp.float32
    )


def gram_both(left, right):
    return lax.dot_general(
        left, right, (((0,), (0,)), ((), ())), precision=HIGH, preferred_element_type=jnp.float32
    )


def eliminate_small(square):
    size_n = square.shape[0]
    augmented = jnp.concatenate([square, jnp.eye(size_n, dtype=square.dtype)], axis=1)
    positions = jnp.arange(size_n)

    def eliminate(pivot, current):
        pivot_row = lax.dynamic_index_in_dim(current, pivot, 0, keepdims=False)
        pivot_row = pivot_row / pivot_row[pivot]
        column = lax.dynamic_index_in_dim(current, pivot, 1, keepdims=False)
        column = column - (positions == pivot).astype(current.dtype)
        return current - column[:, None] * pivot_row[None, :]

    augmented = lax.fori_loop(0, size_n, eliminate, augmented)
    return augmented[:, size_n:]


def invert_square(square):
    size_n = square.shape[0]
    if size_n <= 16:
        return eliminate_small(square)
    half = size_n // 2
    upper_left = square[:half, :half]
    upper_right = square[:half, half:]
    lower_left = square[half:, :half]
    lower_right = square[half:, half:]
    left_inverse = invert_square(upper_left)
    left_times_right = times_of(left_inverse, upper_right)
    lower_times_left = times_of(lower_left, left_inverse)
    schur = lower_right - times_of(lower_left, left_times_right)
    schur_inverse = invert_square(schur)
    top_right = -times_of(left_times_right, schur_inverse)
    bottom_left = -times_of(schur_inverse, lower_times_left)
    top_left = left_inverse - times_of(top_right, lower_times_left)
    upper = jnp.concatenate([top_left, top_right], axis=1)
    lower = jnp.concatenate([bottom_left, schur_inverse], axis=1)
    return jnp.concatenate([upper, lower], axis=0)


def right_solve(factor, values):
    return lax.linalg.triangular_solve(
        factor, values, left_side=False, lower=True, transpose_a=True
    )


def body(panel_block, trailing):
    shard_rows = panel_block.shape[0]
    panel_width = panel_block.shape[1]
    col_count = trailing.shape[1]
    row_index = lax.axis_index("row")
    col_index = lax.axis_index("col")
    first_gram = lax.psum(gram_of(panel_block), "row")
    first_factor = jnp.linalg.cholesky(first_gram)
    first_basis = right_solve(first_factor, panel_block)
    second_gram = lax.psum(gram_of(first_basis), "row")
    second_factor = jnp.linalg.cholesky(second_gram)
    basis = right_solve(second_factor, first_basis)
    top_basis = broadcast(basis[:panel_width], "row", 0)
    band_block = -times_of(second_factor.T, first_factor.T)
    kernel = invert_square(jnp.eye(panel_width, dtype=jnp.float32) + top_basis.T)
    global_rows = row_index * shard_rows + jnp.arange(shard_rows)
    ident = (global_rows[:, None] == jnp.arange(panel_width)[None, :]).astype(jnp.float32)
    vectors = basis + ident
    all_vectors = lax.all_gather(vectors, "row", axis=0, tiled=True)
    col_vectors = lax.dynamic_slice_in_dim(all_vectors, col_index * col_count, col_count, 0)
    partial_product = times_of(trailing, col_vectors)
    row_product = lax.psum(partial_product, "col")
    applied = times_of(row_product, kernel)
    inner_sum = lax.psum(gram_both(vectors, applied), "row")
    inner = times_of(kernel.T, inner_sum)
    row_update = applied - 0.5 * times_of(vectors, inner)
    all_update = lax.all_gather(row_update, "row", axis=0, tiled=True)
    col_update = lax.dynamic_slice_in_dim(all_update, col_index * col_count, col_count, 0)
    reduced = trailing - outer_of(vectors, col_update) - outer_of(row_update, col_vectors)
    return (reduced, band_block, first_factor)


def solution(mesh):
    in_specs = (P("row", None), P("row", "col"))
    out_specs = (P("row", "col"), P(), P())
    return jax.shard_map(body, mesh=mesh, in_specs=in_specs, out_specs=out_specs, check_vma=False)
```

profile of v0, /device:TPU:1, one launch (start us, length us, event | category | flops | bytes accessed | tf_op | source)
XLA Modules:
  0.0 1025.3 jit_solution(8369350252822602380)
XLA Ops:
  9.4 143.5 %all-reduce.6.cloned.1.call-done = f32[128,128]{0,1:T(8,128)} async-done(((f32[128,128]{0,1:T(8,128)}), f32[128,128]{0,1:T(8,128)}) %all-reduce.6.cloned.1.call-update) | async-done | bytes 65552 | tf_op jit(solution)/shard_map/psum | solution.py:86
  154.7 11.7 %cholesky.44 = f32[128,128]{1,0:T(8,128)S(1)} custom-call(f32[128,128]{1,0:T(8,128)S(1)} %fusion.57), custom_call_target="Cholesky" | custom-call | tf_op jit(solution)/shard_map/jit(cholesky)/cholesky | solution.py:87
  167.8 9.8 custom-call.6
  179.3 139.5 %all-reduce.8.cloned.1.call-done = f32[128,128]{0,1:T(8,128)} async-done(((f32[128,128]{0,1:T(8,128)}), f32[128,128]{0,1:T(8,128)}) %all-reduce.8.cloned.1.call-update) | async-done | bytes 65552 | tf_op jit(solution)/shard_map/psum | solution.py:89
  320.6 11.7 %cholesky.55 = f32[128,128]{1,0:T(8,128)S(1)} custom-call(f32[128,128]{1,0:T(8,128)S(1)} %fusion.55), custom_call_target="Cholesky" | custom-call | tf_op jit(solution)/shard_map/jit(cholesky)/cholesky | solution.py:90
  333.5 9.8 custom-call.7
  346.0 138.9 %all-reduce.12.cloned.1.call-done = f32[128,128]{1,0:T(8,128)} async-done(((f32[128,128]{1,0:T(8,128)}), f32[128,128]{1,0:T(8,128)}) %all-reduce.12.cloned.1.call-update) | async-done | bytes 65552 | tf_op jit(solution)/shard_map/psum | solution.py:11
  485.9 24.0 %while.136 = (s32[]{:T(128)}, f32[16,32]{0,1:T(8,128)S(1)}, s32[]{:T(128)}, s32[]{:T(128)}, s32[]{:T(128)}, /*index=5*/s32[]{:T(128)}) while((s32[]{:T(128)}, f32[16,32]{0,1:T(8,128)S(1)}, s32[]{:T(128)}, s32[]{:T(128)}, s32[]{:T(128)}, /*index=5*/s32[]{:T(128)}) %tuple.325), condition=%wide.region_7.10_spmd.clone, body=%wide.region_6.9_spmd.clone.sunk | while | flops 1108 | bytes 5825 | solution.py:48
  510.8 24.0 %while.137 = (s32[]{:T(128)}, f32[16,32]{0,1:T(8,128)S(1)}, s32[]{:T(128)}, s32[]{:T(128)}, s32[]{:T(128)}, /*index=5*/s32[]{:T(128)}) while((s32[]{:T(128)}, f32[16,32]{0,1:T(8,128)S(1)}, s32[]{:T(128)}, s32[]{:T(128)}, s32[]{:T(128)}, /*index=5*/s32[]{:T(128)}) %tuple.328), condition=%wide.region_9.12_spmd.clone, body=%wide.region_8.11_spmd.clone.sunk | while | flops 1108 | bytes 5825 | solution.py:48
  536.2 24.0 %while.138 = (s32[]{:T(128)}, f32[16,32]{0,1:T(8,128)S(1)}, s32[]{:T(128)}, s32[]{:T(128)}, s32[]{:T(128)}, /*index=5*/s32[]{:T(128)}) while((s32[]{:T(128)}, f32[16,32]{0,1:T(8,128)S(1)}, s32[]{:T(128)}, s32[]{:T(128)}, s32[]{:T(128)}, /*index=5*/s32[]{:T(128)}) %tuple.331), condition=%wide.region_11.14_spmd.clone, body=%wide.region_10.13_spmd.clone.sunk | while | flops 1108 | bytes 5825 | solution.py:48
  561.1 24.0 %while.139 = (s32[]{:T(128)}, f32[16,32]{0,1:T(8,128)S(1)}, s32[]{:T(128)}, s32[]{:T(128)}, s32[]{:T(128)}, /*index=5*/s32[]{:T(128)}) while((s32[]{:T(128)}, f32[16,32]{0,1:T(8,128)S(1)}, s32[]{:T(128)}, s32[]{:T(128)}, s32[]{:T(128)}, /*index=5*/s32[]{:T(128)}) %tuple.334), condition=%wide.region_13.16_spmd.clone, body=%wide.region_12.15_spmd.clone.sunk | while | flops 1108 | bytes 5825 | solution.py:48
  587.1 24.0 %while.140 = (s32[]{:T(128)}, f32[16,32]{0,1:T(8,128)S(1)}, s32[]{:T(128)}, s32[]{:T(128)}, s32[]{:T(128)}, /*index=5*/s32[]{:T(128)}) while((s32[]{:T(128)}, f32[16,32]{0,1:T(8,128)S(1)}, s32[]{:T(128)}, s32[]{:T(128)}, s32[]{:T(128)}, /*index=5*/s32[]{:T(128)}) %tuple.337), condition=%wide.region_15.18_spmd.clone, body=%wide.region_14.17_spmd.clone.sunk | while | flops 1108 | bytes 5825 | solution.py:48
  611.7 24.0 %while.141 = (s32[]{:T(128)}, f32[16,32]{0,1:T(8,128)S(1)}, s32[]{:T(128)}, s32[]{:T(128)}, s32[]{:T(128)}, /*index=5*/s32[]{:T(128)}) while((s32[]{:T(128)}, f32[16,32]{0,1:T(8,128)S(1)}, s32[]{:T(128)}, s32[]{:T(128)}, s32[]{:T(128)}, /*index=5*/s32[]{:T(128)}) %tuple.340), condition=%wide.region_17.20_spmd.clone, body=%wide.region_16.19_spmd.clone.sunk | while | flops 1108 | bytes 5825 | solution.py:48
  637.1 24.0 %while.142 = (s32[]{:T(128)}, f32[16,32]{0,1:T(8,128)S(1)}, s32[]{:T(128)}, s32[]{:T(128)}, s32[]{:T(128)}, /*index=5*/s32[]{:T(128)}) while((s32[]{:T(128)}, f32[16,32]{0,1:T(8,128)S(1)}, s32[]{:T(128)}, s32[]{:T(128)}, s32[]{:T(128)}, /*index=5*/s32[]{:T(128)}) %tuple.343), condition=%wide.region_19.22_spmd.clone, body=%wide.region_18.21_spmd.clone.sunk | while | flops 1108 | bytes 5825 | solution.py:48
  661.7 24.0 %while.143 = (s32[]{:T(128)}, f32[16,32]{0,1:T(8,128)S(1)}, s32[]{:T(128)}, s32[]{:T(128)}, s32[]{:T(128)}, /*index=5*/s32[]{:T(128)}) while((s32[]{:T(128)}, f32[16,32]{0,1:T(8,128)S(1)}, s32[]{:T(128)}, s32[]{:T(128)}, s32[]{:T(128)}, /*index=5*/s32[]{:T(128)}) %tuple.346), condition=%wide.region_21.24_spmd.clone, body=%wide.region_20.23_spmd.clone.sunk | while | flops 1108 | bytes 5825 | solution.py:48
  688.1 7.6 convolution_bitcast_fusion
  696.0 65.7 %all-reduce.10.cloned.1.call-done = f32[512,128]{0,1:T(8,128)} async-done(((f32[512,128]{0,1:T(8,128)}), f32[512,128]{0,1:T(8,128)}) %all-reduce.10.cloned.1.call-update) | async-done | bytes 262160 | tf_op jit(solution)/shard_map/psum | solution.py:101
  761.7 1.6 fusion.132
  764.6 139.2 %all-reduce.14.cloned.1.call-done = f32[128,128]{1,0:T(8,128)} async-done(((f32[128,128]{1,0:T(8,128)}), f32[128,128]{1,0:T(8,128)}) %all-reduce.14.cloned.1.call-update) | async-done | bytes 65552 | tf_op jit(solution)/shard_map/psum | solution.py:103
  905.1 1.3 fusion.48
  906.4 1.5 convolution_negate_fusion
  907.9 98.7 %all-gather.5.cloned.1.call-done = f32[16384,128]{1,0:T(8,128)} async-done(((f32[512,128]{1,0:T(8,128)}), f32[16384,128]{1,0:T(8,128)}) %all-gather.5.cloned.1.call-update) | async-done | bytes 8388624 | tf_op jit(solution)/shard_map/all_gather | solution.py:106
  1006.7 5.0 fusion.49
  1011.7 6.7 subtract_subtract_fusion
  (632 shorter events, 217.4 us)
Async XLA Ops:
  7.2 1.0 copy-start
  7.2 145.8 %all-reduce.6.cloned.1.call-start = ((), (), s32[]{:S(2)}) async-start(), calls=%async_computation | async-start | bytes 131072 | tf_op jit(solution)/shard_map/psum | solution.py:86
  9.4 309.4 %all-reduce.8.cloned.1.call-start = ((), (), s32[]{:S(2)}) async-start(), calls=%async_computation.1 | async-start | bytes 131072 | tf_op jit(solution)/shard_map/psum | solution.py:89
  167.8 738.6 %copy-start.4 = (f32[128,128]{1,0:T(8,128)}, f32[128,128]{1,0:T(8,128)S(1)}, u32[]{:S(2)}) copy-start(f32[128,128]{1,0:T(8,128)S(1)} %get-tuple-element.926) | copy-start | bytes 196612
  179.1 305.8 %all-reduce.12.cloned.1.call-start = ((), (), s32[]{:S(2)}) async-start(), calls=%async_computation.4 | async-start | bytes 131072 | tf_op jit(solution)/shard_map/psum | solution.py:11
  345.1 343.0 %all-gather.3.cloned.1.call-start = ((), (), s32[]{:S(2)}) async-start(), calls=%async_computation.2 | async-start | bytes 8650752 | tf_op jit(solution)/shard_map/all_gather | solution.py:98
  345.7 416.0 %all-reduce.10.cloned.1.call-start = ((), (), s32[]{:S(2)}) async-start(), calls=%async_computation.3 | async-start | bytes 524288 | tf_op jit(solution)/shard_map/psum | solution.py:101
  637.1 126.1 %copy-start.2 = (f32[512,128]{0,1:T(8,128)S(1)}, f32[512,128]{0,1:T(8,128)}, u32[]{:S(2)}) copy-start(f32[512,128]{0,1:T(8,128)} %get-tuple-element.927) | copy-start | bytes 786436
  695.7 208.2 %all-reduce.14.cloned.1.call-start = ((), (), s32[]{:S(2)}) async-start(), calls=%async_computation.5 | async-start | bytes 131072 | tf_op jit(solution)/shard_map/psum | solution.py:103
  764.3 242.3 %all-gather.5.cloned.1.call-start = ((), (), s32[]{:S(2)}) async-start(), calls=%async_computation.6 | async-start | bytes 8650752 | tf_op jit(solution)/shard_map/all_gather | solution.py:106
  906.4 105.3 %copy-start.3 = (f32[512,128]{1,0:T(8,128)S(1)}, f32[512,128]{1,0:T(8,128)}, u32[]{:S(2)}) copy-start(f32[512,128]{1,0:T(8,128)} %fusion.48) | copy-start | bytes 786436
  1006.7 5.1 copy-start.1
Sparse Core Ops, SparseCore 0:
  12.0 140.8 all-reduce.5
  179.2 139.5 all-reduce.7
  345.3 139.6 all-reduce.11
  487.9 100.0 all-gather.2
  695.8 65.7 all-reduce.9
  765.6 138.2 all-reduce.13
  907.0 99.5 all-gather.4
where the time goes:
time: 1030 us
  waiting for transfers between devices  726 us (70%)
  other arithmetic  166 us (16%)
  local copies, waits for them, and re-layouts  79.2 us (8%)
  matrix products  37.4 us (4%)
  between operations  14.5 us (1%)
    psum x1, waiting for transfers between devices, body(): first_gram = lax.psum(gram_of(panel_block), 'row')  144 us
    psum x1, waiting for transfers between devices, body(): second_gram = lax.psum(gram_of(first_basis), 'row')  139 us
    psum x1, waiting for transfers between devices, body(): inner_sum = lax.psum(gram_both(vectors, applied), 'row')  139 us
    psum x1, waiting for transfers between devices, broadcast(): return lax.psum(jnp.where(mine, shard, jnp.zeros_like(shard)), axis)  139 us
    div x128, other arithmetic, eliminate(): pivot_row = pivot_row / pivot_row[pivot]  106 us
    all_gather x1, waiting for transfers between devices, body(): all_update = lax.all_gather(row_update, 'row', axis=0, tiled=True)  98.7 us
    dynamic_slice x128, local copies, waits for them, and re-layouts, eliminate(): pivot_row = pivot_row / pivot_row[pivot]  74.9 us
    psum x1, waiting for transfers between devices, body(): row_product = lax.psum(partial_product, 'col')  65.7 us
  transfers between devices with their start and end apart: 7, of which 6 were waited for; matrix products, arithmetic and copies ran while one was open for 20% of the time, Pallas kernels for 0%

commit v1 on v0

--- a/solution.py
+++ b/solution.py
@@ -98,7 +98,12 @@
     all_vectors = lax.all_gather(vectors, "row", axis=0, tiled=True)
     col_vectors = lax.dynamic_slice_in_dim(all_vectors, col_index * col_count, col_count, 0)
     partial_product = times_of(trailing, col_vectors)
-    row_product = lax.psum(partial_product, "col")
+    dev_n = lax.axis_size("col")
+    row_product, mid_arr = (partial_product, 0)
+    while 1 << mid_arr < dev_n:
+        front = lax.ppermute(row_product, "col", [(jj, jj ^ 1 << mid_arr) for jj in range(dev_n)])
+        row_product = row_product + front
+        mid_arr = mid_arr + 1
     applied = times_of(row_product, kernel)
     inner_sum = lax.psum(gram_both(vectors, applied), "row")
     inner = times_of(kernel.T, inner_sum)

time: 1030 us -> 978 us (0.950)
  waiting for transfers between devices: 726 us -> 669 us
    psum x1 -> x0, waiting for transfers between devices: 65.7 us -> none  [body(): row_product = lax.psum(partial_product, 'col')]
    ppermute x0 -> x3, waiting for transfers between devices: none -> 11.7 us  [body(): lax.ppermute(row_product, 'col', [(jj, jj ^ 1 << mid_arr) for jj in range...]
  transfers between devices with their start and end apart: 7 -> 9, of which waited for: 6 -> 8; matrix products, arithmetic and copies ran while one was open for 20% -> 21% of each run, Pallas kernels for 0% -> 0%
where the time goes in v1:
time: 978 us; the launch traced here: 976 us
  waiting for transfers between devices  669 us (68%)
  other arithmetic  166 us (17%)
  local copies, waits for them, and re-layouts  79.2 us (8%)
  matrix products  35.7 us (4%)
  between operations  14.5 us (1%)
  starting transfers between devices  10.1 us (1%)
    psum x1, waiting for transfers between devices, body(): first_gram = lax.psum(gram_of(panel_block), 'row')  144 us
    psum x1, waiting for transfers between devices, body(): second_gram = lax.psum(gram_of(first_basis), 'row')  139 us
    psum x1, waiting for transfers between devices, broadcast(): return lax.psum(jnp.where(mine, shard, jnp.zeros_like(shard)), axis)  139 us
    psum x1, waiting for transfers between devices, body(): inner_sum = lax.psum(gram_both(vectors, applied), 'row')  137 us
    div x128, other arithmetic, eliminate(): pivot_row = pivot_row / pivot_row[pivot]  106 us
    all_gather x1, waiting for transfers between devices, body(): all_update = lax.all_gather(row_update, 'row', axis=0, tiled=True)  98.6 us
    dynamic_slice x128, local copies, waits for them, and re-layouts, eliminate(): pivot_row = pivot_row / pivot_row[pivot]  74.9 us
    another operation x4, other arithmetic, right_solve(): lax.linalg.triangular_solve(factor, values, left_side=False, lower=True,...  20.8 us
  transfers between devices with their start and end apart: 9, of which 8 were waited for; matrix products, arithmetic and copies ran while one was open for 21% of the time, Pallas kernels for 0%

profile of v1, /device:TPU:1, one launch (start us, length us, event | category | flops | bytes accessed | tf_op | source)
XLA Modules:
  0.0 976.0 jit_solution(390528649271397668)
XLA Ops:
  9.4 143.5 %all-reduce.5.cloned.1.call-done = f32[128,128]{0,1:T(8,128)} async-done(((f32[128,128]{0,1:T(8,128)}), f32[128,128]{0,1:T(8,128)}) %all-reduce.5.cloned.1.call-update) | async-done | bytes 65552 | tf_op jit(solution)/shard_map/psum | solution.py:86
  154.7 11.7 %cholesky.44 = f32[128,128]{1,0:T(8,128)S(1)} custom-call(f32[128,128]{1,0:T(8,128)S(1)} %fusion.59), custom_call_target="Cholesky" | custom-call | tf_op jit(solution)/shard_map/jit(cholesky)/cholesky | solution.py:87
  167.8 9.8 %custom-call.6 = f32[1,128,128]{1,2,0:T(8,128)S(1)} custom-call(f32[1,128,128]{2,1,0:T(8,128)S(1)} %get-tuple-element.925), custom_call_target="InvertDiagBlocksLowerTriangular" | custom-call | tf_op jit(solution)/shard_map/triangular_solve/custom-call.0 | solution.py:75
  179.3 139.5 %all-reduce.7.cloned.1.call-done = f32[128,128]{0,1:T(8,128)} async-done(((f32[128,128]{0,1:T(8,128)}), f32[128,128]{0,1:T(8,128)}) %all-reduce.7.cloned.1.call-update) | async-done | bytes 65552 | tf_op jit(solution)/shard_map/psum | solution.py:89
  320.6 11.7 %cholesky.55 = f32[128,128]{1,0:T(8,128)S(1)} custom-call(f32[128,128]{1,0:T(8,128)S(1)} %fusion.57), custom_call_target="Cholesky" | custom-call | tf_op jit(solution)/shard_map/jit(cholesky)/cholesky | solution.py:90
  333.5 9.8 %custom-call.7 = f32[1,128,128]{1,2,0:T(8,128)S(1)} custom-call(f32[1,128,128]{2,1,0:T(8,128)S(1)} %select_bitcast_fusion), custom_call_target="InvertDiagBlocksLowerTriangular" | custom-call | tf_op jit(solution)/shard_map/triangular_solve/custom-call.0 | solution.py:75
  346.0 138.9 %all-reduce.9.cloned.1.call-done = f32[128,128]{1,0:T(8,128)} async-done(((f32[128,128]{1,0:T(8,128)}), f32[128,128]{1,0:T(8,128)}) %all-reduce.9.cloned.1.call-update) | async-done | bytes 65552 | tf_op jit(solution)/shard_map/psum | solution.py:11
  485.9 24.0 %while.136 = (s32[]{:T(128)}, f32[16,32]{0,1:T(8,128)S(1)}, s32[]{:T(128)}, s32[]{:T(128)}, s32[]{:T(128)}, /*index=5*/s32[]{:T(128)}) while((s32[]{:T(128)}, f32[16,32]{0,1:T(8,128)S(1)}, s32[]{:T(128)}, s32[]{:T(128)}, s32[]{:T(128)}, /*index=5*/s32[]{:T(128)}) %tuple.325), condition=%wide.region_6.9_spmd.clone, body=%wide.region_5.8_spmd.clone.sunk | while | flops 1108 | bytes 5825 | solution.py:48
  510.8 24.0 %while.137 = (s32[]{:T(128)}, f32[16,32]{0,1:T(8,128)S(1)}, s32[]{:T(128)}, s32[]{:T(128)}, s32[]{:T(128)}, /*index=5*/s32[]{:T(128)}) while((s32[]{:T(128)}, f32[16,32]{0,1:T(8,128)S(1)}, s32[]{:T(128)}, s32[]{:T(128)}, s32[]{:T(128)}, /*index=5*/s32[]{:T(128)}) %tuple.328), condition=%wide.region_8.11_spmd.clone, body=%wide.region_7.10_spmd.clone.sunk | while | flops 1108 | bytes 5825 | solution.py:48
  536.2 24.0 %while.138 = (s32[]{:T(128)}, f32[16,32]{0,1:T(8,128)S(1)}, s32[]{:T(128)}, s32[]{:T(128)}, s32[]{:T(128)}, /*index=5*/s32[]{:T(128)}) while((s32[]{:T(128)}, f32[16,32]{0,1:T(8,128)S(1)}, s32[]{:T(128)}, s32[]{:T(128)}, s32[]{:T(128)}, /*index=5*/s32[]{:T(128)}) %tuple.331), condition=%wide.region_10.13_spmd.clone, body=%wide.region_9.12_spmd.clone.sunk | while | flops 1108 | bytes 5825 | solution.py:48
  561.1 24.0 %while.139 = (s32[]{:T(128)}, f32[16,32]{0,1:T(8,128)S(1)}, s32[]{:T(128)}, s32[]{:T(128)}, s32[]{:T(128)}, /*index=5*/s32[]{:T(128)}) while((s32[]{:T(128)}, f32[16,32]{0,1:T(8,128)S(1)}, s32[]{:T(128)}, s32[]{:T(128)}, s32[]{:T(128)}, /*index=5*/s32[]{:T(128)}) %tuple.334), condition=%wide.region_12.15_spmd.clone, body=%wide.region_11.14_spmd.clone.sunk | while | flops 1108 | bytes 5825 | solution.py:48
  587.1 24.0 %while.140 = (s32[]{:T(128)}, f32[16,32]{0,1:T(8,128)S(1)}, s32[]{:T(128)}, s32[]{:T(128)}, s32[]{:T(128)}, /*index=5*/s32[]{:T(128)}) while((s32[]{:T(128)}, f32[16,32]{0,1:T(8,128)S(1)}, s32[]{:T(128)}, s32[]{:T(128)}, s32[]{:T(128)}, /*index=5*/s32[]{:T(128)}) %tuple.337), condition=%wide.region_14.17_spmd.clone, body=%wide.region_13.16_spmd.clone.sunk | while | flops 1108 | bytes 5825 | solution.py:48
  611.7 24.0 %while.141 = (s32[]{:T(128)}, f32[16,32]{0,1:T(8,128)S(1)}, s32[]{:T(128)}, s32[]{:T(128)}, s32[]{:T(128)}, /*index=5*/s32[]{:T(128)}) while((s32[]{:T(128)}, f32[16,32]{0,1:T(8,128)S(1)}, s32[]{:T(128)}, s32[]{:T(128)}, s32[]{:T(128)}, /*index=5*/s32[]{:T(128)}) %tuple.340), condition=%wide.region_16.19_spmd.clone, body=%wide.region_15.18_spmd.clone.sunk | while | flops 1108 | bytes 5825 | solution.py:48
  637.1 24.0 %while.142 = (s32[]{:T(128)}, f32[16,32]{0,1:T(8,128)S(1)}, s32[]{:T(128)}, s32[]{:T(128)}, s32[]{:T(128)}, /*index=5*/s32[]{:T(128)}) while((s32[]{:T(128)}, f32[16,32]{0,1:T(8,128)S(1)}, s32[]{:T(128)}, s32[]{:T(128)}, s32[]{:T(128)}, /*index=5*/s32[]{:T(128)}) %tuple.343), condition=%wide.region_18.21_spmd.clone, body=%wide.region_17.20_spmd.clone.sunk | while | flops 1108 | bytes 5825 | solution.py:48
  661.7 24.0 %while.143 = (s32[]{:T(128)}, f32[16,32]{0,1:T(8,128)S(1)}, s32[]{:T(128)}, s32[]{:T(128)}, s32[]{:T(128)}, /*index=5*/s32[]{:T(128)}) while((s32[]{:T(128)}, f32[16,32]{0,1:T(8,128)S(1)}, s32[]{:T(128)}, s32[]{:T(128)}, s32[]{:T(128)}, /*index=5*/s32[]{:T(128)}) %tuple.346), condition=%wide.region_20.23_spmd.clone, body=%wide.region_19.22_spmd.clone.sunk | while | flops 1108 | bytes 5825 | solution.py:48
  687.2 6.9 convolution_bitcast_fusion
  694.1 5.0 collective-permute-start
  702.0 5.9 collective-permute-done.1
  707.9 2.8 collective-permute-start.2
  711.2 5.0 collective-permute-done.2
  718.2 136.5 %all-reduce.11.cloned.1.call-done = f32[128,128]{1,0:T(8,128)} async-done(((f32[128,128]{1,0:T(8,128)}), f32[128,128]{1,0:T(8,128)}) %all-reduce.11.cloned.1.call-update) | async-done | bytes 65552 | tf_op jit(solution)/shard_map/psum | solution.py:108
  858.8 98.6 %all-gather.5.cloned.1.call-done = f32[16384,128]{1,0:T(8,128)} async-done(((f32[512,128]{1,0:T(8,128)}), f32[16384,128]{1,0:T(8,128)}) %all-gather.5.cloned.1.call-update) | async-done | bytes 8388624 | tf_op jit(solution)/shard_map/all_gather | solution.py:111
  957.4 5.0 fusion.49
  962.4 6.7 subtract_subtract_fusion
  (637 shorter events, 223.0 us)
Async XLA Ops:
  7.2 1.0 copy-start
  7.2 145.8 %all-reduce.5.cloned.1.call-start = ((), (), s32[]{:S(2)}) async-start(), calls=%async_computation | async-start | bytes 131072 | tf_op jit(solution)/shard_map/psum | solution.py:86
  9.4 309.4 %all-reduce.7.cloned.1.call-start = ((), (), s32[]{:S(2)}) async-start(), calls=%async_computation.1 | async-start | bytes 131072 | tf_op jit(solution)/shard_map/psum | solution.py:89
  167.8 689.5 %copy-start.4 = (f32[128,128]{1,0:T(8,128)}, f32[128,128]{1,0:T(8,128)S(1)}, u32[]{:S(2)}) copy-start(f32[128,128]{1,0:T(8,128)S(1)} %get-tuple-element.926) | copy-start | bytes 196612
  179.1 305.8 %all-reduce.9.cloned.1.call-start = ((), (), s32[]{:S(2)}) async-start(), calls=%async_computation.3 | async-start | bytes 131072 | tf_op jit(solution)/shard_map/psum | solution.py:11
  345.1 342.0 %all-gather.3.cloned.1.call-start = ((), (), s32[]{:S(2)}) async-start(), calls=%async_computation.2 | async-start | bytes 8650752 | tf_op jit(solution)/shard_map/all_gather | solution.py:98
  345.7 509.0 %all-reduce.11.cloned.1.call-start = ((), (), s32[]{:S(2)}) async-start(), calls=%async_computation.4 | async-start | bytes 131072 | tf_op jit(solution)/shard_map/psum | solution.py:108
  687.1 29.7 %copy-start.2 = (f32[512,128]{0,1:T(8,128)S(1)}, f32[512,128]{0,1:T(8,128)}, u32[]{:S(2)}) copy-start(f32[512,128]{0,1:T(8,128)} %get-tuple-element.927) | copy-start | bytes 786436
  694.1 6.2 collective-permute-start
  700.3 7.6 collective-permute-start.1
  707.9 8.2 collective-permute-start.2
  717.9 239.5 %all-gather.5.cloned.1.call-start = ((), (), s32[]{:S(2)}) async-start(), calls=%async_computation.5 | async-start | bytes 8650752 | tf_op jit(solution)/shard_map/all_gather | solution.py:111
  857.2 105.2 %copy-start.3 = (f32[512,128]{1,0:T(8,128)S(1)}, f32[512,128]{1,0:T(8,128)}, u32[]{:S(2)}) copy-start(f32[512,128]{1,0:T(8,128)} %fusion.48) | copy-start | bytes 786436
  957.4 5.1 copy-start.1
Sparse Core Ops, SparseCore 0:
  12.0 140.8 all-reduce.4
  179.2 139.5 all-reduce.6
  345.3 139.6 all-reduce.8
  487.9 100.0 all-gather.2
  718.0 136.6 all-reduce.10
  857.7 99.5 all-gather.4
